TPU v7x, 128 devices: a whole 4x4x4 slice. The times are simulated.
128 devices in a mesh: ex: 16 (over z, y), feat: 8 (over x, core).
Axes of the slice: x: 4, y: 4, z: 4, core: 2. Of those that a mesh axis runs over, the one named last changes fastest.
Arguments:
- tiles: bfloat16 [16, 8, 384, 128, 128], P('ex', 'feat'), may hold values from -0.5 to 0.5
- row_index: int32 [16, 8, 384], P('ex', 'feat'), may hold values from 0 to 2047
- col_index: int32 [16, 8, 384], P('ex', 'feat'), may hold values from 0 to 4095
- weights: bfloat16 [32768, 128], P('feat'), may hold values from -6 to 6
- val_grad: float32 [32768, 128], P('feat'), may hold values from -6 to 6
- field_map: int32 [32768, 128], P('feat'), may hold values from 0 to 63
- field_lambda: float32 [64], replicated, may hold values from 0.05 to 2
Outputs:
- solution: float32 [32768, 128], P(('feat', 'ex'))
- hypergrad: float32 [64], replicated
Inputs may be any that keep to these rules, and one draw needn't show every extreme that they name: `row_index`: local row tile of a stored tile within its device's 2048 row tiles. `col_index`: local column tile of a stored tile within its device's 4096 column tiles.
All inputs are finite; a program needn't handle non-finite values.
Results may differ from a plain program's by a relative error of at most 0.0021.
Values may be sent and summed in bfloat16 or wider, within the bound.
A program may use at most 128 MiB of HBM per device.

v0:
```python
import math
import jax
import jax.numpy as jnp
from jax import lax
from jax.sharding import PartitionSpec as P

RT_DEV = 2048
ITERS = 3


def on_device(tiles, row_index, col_index, weights, val_grad, field_map, field_lambda):
    tile_count = tiles.shape[2]
    tile_width = tiles.shape[3]
    tile_stack = tiles.reshape(tile_count, tile_width, tile_width)
    row_ids = row_index.reshape(tile_count)
    col_ids = col_index.reshape(tile_count)
    segment = weights.shape[0]
    share_len = segment // lax.axis_size("ex")
    offset = lax.axis_index("ex") * share_len
    field_count = field_lambda.shape[0]
    labels = jnp.arange(field_count, dtype=jnp.int32)
    norm_scale = 1.0 / math.sqrt(segment * tile_width * lax.axis_size("feat") // field_count)

    def own_part(vector):
        return lax.dynamic_slice_in_dim(vector, offset, share_len, 0)

    def forward(vec_b):
        pieces = jnp.take(vec_b, col_ids, axis=0)
        products = jnp.einsum("tij,tj->ti", tile_stack, pieces, preferred_element_type=jnp.float32)
        partial_rows = jnp.zeros((RT_DEV, tile_width), jnp.float32).at[row_ids].add(products)
        return lax.psum(partial_rows, "feat")

    def lookup(field_block):
        matches = field_block[..., None] == labels
        return jnp.sum(jnp.where(matches, field_lambda, 0.0), axis=-1)

    margin = forward(weights)
    prob = jax.nn.sigmoid(margin)
    curv_weight = prob * (1.0 - prob)
    count = field_map.shape[0]
    block_rows = math.gcd(count, 256)
    lam_part = lax.map(lookup, field_map.reshape(-1, block_rows, tile_width)).reshape(
        count, tile_width
    )
    residual = val_grad

    def local(vector):
        return own_part(vector)

    direction = residual
    solution = jnp.zeros_like(residual)
    dir_b = val_grad.astype(jnp.bfloat16)
    mine = local(residual)
    norm_now = lax.psum(jnp.sum(mine * mine), ("ex", "feat"))
    for step in range(ITERS):
        rows_sum = forward(dir_b)
        scaled_part = (curv_weight * rows_sum).astype(jnp.bfloat16)
        backward_pieces = jnp.take(scaled_part, row_ids, axis=0)
        backward_products = jnp.einsum(
            "tij,ti->tj", tile_stack, backward_pieces, preferred_element_type=jnp.float32
        )
        partial_feat = (
            jnp.zeros((segment, tile_width), jnp.float32).at[col_ids].add(backward_products)
        )
        image = lax.psum(partial_feat, "ex") + lam_part * direction
        own_dir = local(direction)
        own_image = local(image)
        curv_sum = lax.psum(jnp.sum(own_dir * own_image), ("ex", "feat"))
        step_size = norm_now / curv_sum
        solution = solution + step_size * direction
        residual = residual - step_size * image
        if step + 1 < ITERS:
            own_res = local(residual)
            next_norm = lax.psum(jnp.sum(own_res * own_res), ("ex", "feat"))
        if step + 1 < ITERS:
            direction = residual + next_norm / norm_now * direction
            norm_now = next_norm
            dir_b = direction.astype(jnp.bfloat16)
    own_solution = local(solution)
    own_terms = own_solution * own_part(weights).astype(jnp.float32)
    own_fields = own_part(field_map)
    share_block = math.gcd(share_len, 256)

    def field_sums(element):
        term_block, field_block = element
        matches = field_block[..., None] == labels
        return jnp.sum(jnp.where(matches, term_block[..., None], 0.0), axis=(0, 1))

    per_block = lax.map(
        field_sums,
        (
            own_terms.reshape(-1, share_block, tile_width),
            own_fields.reshape(-1, share_block, tile_width),
        ),
    )
    totals = lax.psum(jnp.sum(per_block, axis=0), ("ex", "feat"))
    hypergrad = -field_lambda * totals * norm_scale
    return (own_solution, hypergrad)


def solution(mesh):
    return jax.shard_map(
        on_device,
        mesh=mesh,
        in_specs=(
            P("ex", "feat", None, None, None),
            P("ex", "feat", None),
            P("ex", "feat", None),
            P("feat", None),
            P("feat", None),
            P("feat", None),
            P(),
        ),
        out_specs=(P(("feat", "ex"), None), P()),
        check_vma=False,
    )
```

profile of v0, /device:TPU:1, one launch (start us, length us, event | category | flops | bytes accessed | tf_op | source)
XLA Modules:
  0.0 994.2 jit_solution(16957785030988315214)
XLA Ops:
  8.1 1.7 convert_element_type.21
  9.8 1.4 gather_fusion.1
  11.2 1.4 gather_fusion
  12.9 10.9 %fusion.14 = f32[384,1,128]{2,1,0:T(1,128)S(1)} fusion(bf16[1,1,384,128,128]{4,3,2,1,0:T(8,128)(2,1)} %param.13, bf16[384,128,1]{1,0,2:T(8,128)(2,1)S(1)} %get-tuple-element.77), kind=kOutput, calls=%fused_computation.31 | convolution fusion | flops 12582912 | bytes 12877824 | tf_op jit(solution)/shard_map/tij,tj->ti/dot_general | solution.py:29
  23.8 6.6 fusion.12
  30.4 2.9 scatter_custom_fusion
  33.3 2.8 scatter_custom_fusion.1
  36.7 66.6 %all-reduce.19.cloned.1.call-done = (f32[2048,128]{1,0:T(8,128)}, f32[2048,128]{1,0:T(8,128)}) async-done(((f32[2048,128]{1,0:T(8,128)}, f32[2048,128]{1,0:T(8,128)}), (f32[2048,128]{1,0:T(8,128)}, f32[2048,128]{1,0:T(8,128)})) %all-reduce.19.cloned.1.call-update) | async-done | bytes 2097168 | tf_op jit(solution)/shard_map/psum | solution.py:31
  103.3 1.9 multiply_convert_fusion.2
  106.7 6.4 fusion.10
  113.1 3.2 scatter_custom_fusion.2
  116.4 71.8 %while.3 = (s32[]{:T(128)}, f32[16,256,128]{2,1,0:T(8,128)}, s32[16,256,128]{2,1,0:T(8,128)}, f32[64]{0:T(128)S(1)}, s32[]{:T(128)}) while((s32[]{:T(128)}, f32[16,256,128]{2,1,0:T(8,128)}, s32[16,256,128]{2,1,0:T(8,128)}, f32[64]{0:T(128)S(1)}, s32[]{:T(128)}) %tuple.52), condition=%wide.region_10.13_spmd.clone, body=%wide.region_8.12_spmd.clone.sunk | while | flops 6258690 | bytes 787265 | solution.py:42
  117.5 2.9 select_reduce_fusion.3
  121.9 2.9 select_reduce_fusion.3
  126.4 2.9 select_reduce_fusion.3
  130.9 2.9 select_reduce_fusion.3
  135.4 2.9 select_reduce_fusion.3
  139.9 2.9 select_reduce_fusion.3
  144.3 2.9 select_reduce_fusion.3
  148.8 2.9 select_reduce_fusion.3
  153.3 2.9 select_reduce_fusion.3
  157.8 2.9 select_reduce_fusion.3
  162.2 2.9 select_reduce_fusion.3
  166.7 2.9 select_reduce_fusion.3
  171.2 2.9 select_reduce_fusion.3
  175.7 2.9 select_reduce_fusion.3
  180.2 2.9 select_reduce_fusion.3
  184.7 2.9 select_reduce_fusion.3
  188.2 19.2 %all-reduce.9.cloned.1.call-done = f32[4096,128]{1,0:T(8,128)} async-done(((f32[4096,128]{1,0:T(8,128)}), f32[4096,128]{1,0:T(8,128)}) %all-reduce.9.cloned.1.call-update) | async-done | bytes 2097168 | tf_op jit(solution)/shard_map/psum | solution.py:65
  207.4 3.9 multiply_add_fusion.3
  211.2 1.5 multiply_reduce_fusion.3
  212.8 65.3 %all-reduce = (f32[]{:T(128)}, f32[]{:T(128)}) all-reduce(f32[]{:T(128)} %get-tuple-element.58, f32[]{:T(128)} %get-tuple-element.57), channel_id=1, replica_groups=mesh['ex'=16,'feat'=8] {'ex','feat'}, use_global_device_ids=true, to_apply=%region_1.2 | all-reduce | flops 2 | bytes 16 | tf_op jit(solution)/shard_map/psum | solution.py:54
  279.5 3.1 multiply_subtract_fusion.1
  282.6 1.5 multiply_reduce_fusion.2
  284.2 62.7 %psum.103 = f32[]{:T(128)} all-reduce(f32[]{:T(128)} %multiply_reduce_fusion.2), channel_id=1, replica_groups=mesh['ex'=16,'feat'=8] {'ex','feat'}, use_global_device_ids=true, to_apply=%region_14.17 | all-reduce | flops 1 | bytes 8 | tf_op jit(solution)/shard_map/psum | solution.py:74
  348.2 3.2 fusion.42
  353.0 9.5 fusion.8
  362.5 2.9 scatter_custom_fusion.3
  365.4 57.4 %all-reduce.11.cloned.1.call-done = f32[2048,128]{1,0:T(8,128)} async-done(((f32[2048,128]{1,0:T(8,128)}), f32[2048,128]{1,0:T(8,128)}) %all-reduce.11.cloned.1.call-update) | async-done | bytes 1048592 | tf_op jit(solution)/shard_map/psum | solution.py:31
  422.8 2.4 multiply_convert_fusion.1
  425.2 2.3 gather_fusion.4
  427.6 6.4 fusion.6
  434.0 3.3 scatter_custom_fusion.4
  437.4 90.8 %all-reduce.13.cloned.1.call-done = f32[4096,128]{1,0:T(8,128)} async-done(((f32[4096,128]{1,0:T(8,128)}), f32[4096,128]{1,0:T(8,128)}) %all-reduce.13.cloned.1.call-update) | async-done | bytes 2097168 | tf_op jit(solution)/shard_map/psum | solution.py:65
  528.1 3.2 multiply_add_fusion.1
  532.6 1.5 multiply_reduce_fusion.1
  534.1 65.4 %psum.106 = f32[]{:T(128)} all-reduce(f32[]{:T(128)} %multiply_reduce_fusion.1), channel_id=1, replica_groups=mesh['ex'=16,'feat'=8] {'ex','feat'}, use_global_device_ids=true, to_apply=%region_20.23 | all-reduce | flops 1 | bytes 8 | tf_op jit(solution)/shard_map/psum | solution.py:68
  600.8 2.4 multiply_subtract_fusion
  605.2 62.8 %psum.107 = f32[]{:T(128)} all-reduce(f32[]{:T(128)} %multiply_reduce_fusion), channel_id=1, replica_groups=mesh['ex'=16,'feat'=8] {'ex','feat'}, use_global_device_ids=true, to_apply=%region_22.25 | all-reduce | flops 1 | bytes 8 | tf_op jit(solution)/shard_map/psum | solution.py:74
  669.3 4.3 fusion.41
  673.6 2.5 gather_fusion.5
  676.3 9.5 fusion.4
  685.7 2.9 scatter_custom_fusion.5
  688.6 57.5 %all-reduce.15.cloned.1.call-done = f32[2048,128]{1,0:T(8,128)} async-done(((f32[2048,128]{1,0:T(8,128)}), f32[2048,128]{1,0:T(8,128)}) %all-reduce.15.cloned.1.call-update) | async-done | bytes 1048592 | tf_op jit(solution)/shard_map/psum | solution.py:31
  746.2 2.4 multiply_convert_fusion
  748.5 2.3 gather_fusion.6
  750.9 6.4 fusion.2
  757.3 3.3 scatter_custom_fusion.6
  760.6 90.9 %all-reduce.17.cloned.1.call-done = f32[4096,128]{1,0:T(8,128)} async-done(((f32[4096,128]{1,0:T(8,128)}), f32[4096,128]{1,0:T(8,128)}) %all-reduce.17.cloned.1.call-update) | async-done | bytes 2097168 | tf_op jit(solution)/shard_map/psum | solution.py:65
  851.5 1.7 fusion.38
  854.1 65.4 %psum.110 = f32[]{:T(128)} all-reduce(f32[]{:T(128)} %fusion.38), channel_id=1, replica_groups=mesh['ex'=16,'feat'=8] {'ex','feat'}, use_global_device_ids=true, to_apply=%region_28.31 | all-reduce | flops 1 | bytes 8 | tf_op jit(solution)/shard_map/psum | solution.py:68
  920.9 1.7 convert_multiply_fusion
  922.6 1.5 select_reduce_fusion.1
  924.1 62.6 %psum.111 = f32[64]{0:T(128)S(1)} all-reduce(f32[64]{0:T(128)S(1)} %select_reduce_fusion.1), channel_id=1, replica_groups=mesh['ex'=16,'feat'=8] {'ex','feat'}, use_global_device_ids=true, to_apply=%region_30.33 | all-reduce | flops 64 | bytes 512 | tf_op jit(solution)/shard_map/psum | solution.py:96
  (83 shorter events, 35.4 us)
Async XLA Ops:
  7.2 4.1 copy-start.5
  7.2 96.1 %all-reduce.19.cloned.1.call-start = ((), (), s32[]{:S(2)}) async-start(), calls=%async_computation.5 | async-start | bytes 4194304 | tf_op jit(solution)/shard_map/psum | solution.py:31
  8.0 4.7 copy-start.7
  8.0 4.7 copy-start.8
  12.9 10.9 %copy-start = (bf16[1,1,384,128,128]{4,3,2,1,0:T(8,128)(2,1)S(1)}, bf16[1,1,384,128,128]{4,3,2,1,0:T(8,128)(2,1)}, u32[]{:S(2)}) copy-start(bf16[1,1,384,128,128]{4,3,2,1,0:T(8,128)(2,1)} %param.13) | copy-start | bytes 37748740
  36.1 171.3 %all-reduce.9.cloned.1.call-start = ((), (), s32[]{:S(2)}) async-start(), calls=%async_computation | async-start | bytes 4194304 | tf_op jit(solution)/shard_map/psum | solution.py:65
  113.1 3.3 copy-start.6
  116.3 91.1 %copy-start.1 = (f32[4096,128]{1,0:T(8,128)S(1)}, f32[4096,128]{1,0:T(8,128)}, u32[]{:S(2)}) copy-start(f32[4096,128]{1,0:T(8,128)} %param.17) | copy-start | bytes 6291460
  116.3 306.5 %all-reduce.11.cloned.1.call-start = ((), (), s32[]{:S(2)}) async-start(), calls=%async_computation.1 | async-start | bytes 2097152 | tf_op jit(solution)/shard_map/psum | solution.py:31
  362.5 60.4 %copy-start.2 = (f32[2048,128]{1,0:T(8,128)S(1)}, f32[2048,128]{1,0:T(8,128)}, u32[]{:S(2)}) copy-start(f32[2048,128]{1,0:T(8,128)} %get-tuple-element.70) | copy-start | bytes 3145732
  365.4 162.8 %all-reduce.13.cloned.1.call-start = ((), (), s32[]{:S(2)}) async-start(), calls=%async_computation.2 | async-start | bytes 4194304 | tf_op jit(solution)/shard_map/psum | solution.py:65
  437.3 308.8 %all-reduce.15.cloned.1.call-start = ((), (), s32[]{:S(2)}) async-start(), calls=%async_computation.3 | async-start | bytes 2097152 | tf_op jit(solution)/shard_map/psum | solution.py:31
  531.3 1.3 copy-start.4
  603.3 1.3 copy-start.3
  688.6 162.9 %all-reduce.17.cloned.1.call-start = ((), (), s32[]{:S(2)}) async-start(), calls=%async_computation.4 | async-start | bytes 4194304 | tf_op jit(solution)/shard_map/psum | solution.py:65
Sparse Core Ops, SparseCore 0:
  36.2 66.9 all-reduce.18
  116.5 90.8 all-reduce.8
  365.5 57.3 all-reduce.10
  437.4 90.6 all-reduce.12
  688.7 57.3 all-reduce.14
  760.8 90.7 all-reduce.16
where the time goes:
time: 1000 us; the launch traced here: 994 us
  blocking collectives  384 us (38%)
  waiting for transfers between devices  382 us (38%)
  other arithmetic  108 us (11%)
  matrix products  55.5 us (6%)
  local copies, waits for them, and re-layouts  41.8 us (4%)
  between operations  21.3 us (2%)
    psum x3, waiting for transfers between devices, on_device(): image = lax.psum(partial_feat, 'ex') + lam_part * direction  201 us
    psum x3, waiting for transfers between devices, forward(): return lax.psum(partial_rows, 'feat')  182 us
    psum x2, blocking collectives, on_device(): curv_sum = lax.psum(jnp.sum(own_dir * own_image), ('ex', 'feat'))  131 us
    psum x2, blocking collectives, on_device(): next_norm = lax.psum(jnp.sum(own_res * own_res), ('ex', 'feat'))  125 us
    psum x1, blocking collectives, on_device(): norm_now = lax.psum(jnp.sum(mine * mine), ('ex', 'feat'))  65.3 us
    psum x1, blocking collectives, on_device(): totals = lax.psum(jnp.sum(per_block, axis=0), ('ex', 'feat'))  62.6 us
    reduce_sum x16, other arithmetic, lookup(): return jnp.sum(jnp.where(matches, field_lambda, 0.0), axis=-1)  46.3 us
    dot_general x4, matrix products, forward(): jnp.einsum('tij,tj->ti', tile_stack, pieces, preferred_element_type=jnp.f...  36.4 us
  transfers between devices with their start and end apart: 6, of which 6 were waited for; matrix products, arithmetic and copies ran while one was open for 7% of the time, Pallas kernels for 0%

commit v1 on v0

--- a/solution.py
+++ b/solution.py
@@ -93,7 +93,9 @@
             own_fields.reshape(-1, share_block, tile_width),
         ),
     )
-    totals = lax.psum(jnp.sum(per_block, axis=0), ("ex", "feat"))
+    totals = jnp.sum(per_block, axis=0)
+    for axis in ("feat", "ex"):
+        totals = lax.psum(totals, axis)
     hypergrad = -field_lambda * totals * norm_scale
     return (own_solution, hypergrad)
 

time: 1000 us -> 989 us (0.989)
  blocking collectives: 384 us -> 365 us
    psum x1 -> x2, blocking collectives: 62.6 us -> 43.5 us  [on_device(): totals = lax.psum(totals, axis)]
where the time goes in v1:
time: 989 us; the launch traced here: 975 us
  waiting for transfers between devices  382 us (39%)
  blocking collectives  365 us (37%)
  other arithmetic  108 us (11%)
  matrix products  55.5 us (6%)
  local copies, waits for them, and re-layouts  41.8 us (4%)
  between operations  21.3 us (2%)
    psum x3, waiting for transfers between devices, on_device(): image = lax.psum(partial_feat, 'ex') + lam_part * direction  201 us
    psum x3, waiting for transfers between devices, forward(): return lax.psum(partial_rows, 'feat')  182 us
    psum x2, blocking collectives, on_device(): curv_sum = lax.psum(jnp.sum(own_dir * own_image), ('ex', 'feat'))  131 us
    psum x2, blocking collectives, on_device(): next_norm = lax.psum(jnp.sum(own_res * own_res), ('ex', 'feat'))  125 us
    psum x1, blocking collectives, on_device(): norm_now = lax.psum(jnp.sum(mine * mine), ('ex', 'feat'))  65.3 us
    reduce_sum x16, other arithmetic, lookup(): return jnp.sum(jnp.where(matches, field_lambda, 0.0), axis=-1)  46.3 us
    psum x2, blocking collectives, on_device(): totals = lax.psum(totals, axis)  43.5 us
    dot_general x4, matrix products, forward(): jnp.einsum('tij,tj->ti', tile_stack, pieces, preferred_element_type=jnp.f...  36.4 us
  transfers between devices with their start and end apart: 6, of which 6 were waited for; matrix products, arithmetic and copies ran while one was open for 7% of the time, Pallas kernels for 0%

profile of v1, /device:TPU:1, one launch (start us, length us, event | category | flops | bytes accessed | tf_op | source)
XLA Modules:
  0.0 975.2 jit_solution(17446023334320487343)
XLA Ops:
  8.1 1.7 convert_element_type.21
  11.2 1.4 gather_fusion
  12.9 10.9 %fusion.14 = f32[384,1,128]{2,1,0:T(1,128)S(1)} fusion(bf16[1,1,384,128,128]{4,3,2,1,0:T(8,128)(2,1)} %param.13, bf16[384,128,1]{1,0,2:T(8,128)(2,1)S(1)} %get-tuple-element.77), kind=kOutput, calls=%fused_computation.31 | convolution fusion | flops 12582912 | bytes 12877824 | tf_op jit(solution)/shard_map/tij,tj->ti/dot_general | solution.py:29
  23.8 6.6 fusion.12
  30.4 2.9 scatter_custom_fusion
  33.3 2.8 scatter_custom_fusion.1
  36.7 66.6 %all-reduce.19.cloned.1.call-done = (f32[2048,128]{1,0:T(8,128)}, f32[2048,128]{1,0:T(8,128)}) async-done(((f32[2048,128]{1,0:T(8,128)}, f32[2048,128]{1,0:T(8,128)}), (f32[2048,128]{1,0:T(8,128)}, f32[2048,128]{1,0:T(8,128)})) %all-reduce.19.cloned.1.call-update) | async-done | bytes 2097168 | tf_op jit(solution)/shard_map/psum | solution.py:31
  103.3 1.9 multiply_convert_fusion.2
  106.7 6.4 fusion.10
  113.1 3.2 scatter_custom_fusion.2
  116.4 71.8 %while.3 = (s32[]{:T(128)}, f32[16,256,128]{2,1,0:T(8,128)}, s32[16,256,128]{2,1,0:T(8,128)}, f32[64]{0:T(128)S(1)}, s32[]{:T(128)}) while((s32[]{:T(128)}, f32[16,256,128]{2,1,0:T(8,128)}, s32[16,256,128]{2,1,0:T(8,128)}, f32[64]{0:T(128)S(1)}, s32[]{:T(128)}) %tuple.52), condition=%wide.region_10.13_spmd.clone, body=%wide.region_8.12_spmd.clone.sunk | while | flops 6258690 | bytes 787265 | solution.py:42
  117.5 2.9 select_reduce_fusion.3
  121.9 2.9 select_reduce_fusion.3
  126.4 2.9 select_reduce_fusion.3
  130.9 2.9 select_reduce_fusion.3
  135.4 2.9 select_reduce_fusion.3
  139.9 2.9 select_reduce_fusion.3
  144.3 2.9 select_reduce_fusion.3
  148.8 2.9 select_reduce_fusion.3
  153.3 2.9 select_reduce_fusion.3
  157.8 2.9 select_reduce_fusion.3
  162.2 2.9 select_reduce_fusion.3
  166.7 2.9 select_reduce_fusion.3
  171.2 2.9 select_reduce_fusion.3
  175.7 2.9 select_reduce_fusion.3
  180.2 2.9 select_reduce_fusion.3
  184.7 2.9 select_reduce_fusion.3
  188.2 19.2 %all-reduce.9.cloned.1.call-done = f32[4096,128]{1,0:T(8,128)} async-done(((f32[4096,128]{1,0:T(8,128)}), f32[4096,128]{1,0:T(8,128)}) %all-reduce.9.cloned.1.call-update) | async-done | bytes 2097168 | tf_op jit(solution)/shard_map/psum | solution.py:65
  207.4 3.9 multiply_add_fusion.3
  211.2 1.5 multiply_reduce_fusion.3
  212.8 65.3 %all-reduce = (f32[]{:T(128)}, f32[]{:T(128)}) all-reduce(f32[]{:T(128)} %get-tuple-element.58, f32[]{:T(128)} %get-tuple-element.57), channel_id=1, replica_groups=mesh['ex'=16,'feat'=8] {'ex','feat'}, use_global_device_ids=true, to_apply=%region_1.2 | all-reduce | flops 2 | bytes 16 | tf_op jit(solution)/shard_map/psum | solution.py:54
  279.5 3.1 multiply_subtract_fusion.1
  282.6 1.5 multiply_reduce_fusion.2
  284.2 62.7 %psum.110 = f32[]{:T(128)} all-reduce(f32[]{:T(128)} %multiply_reduce_fusion.2), channel_id=1, replica_groups=mesh['ex'=16,'feat'=8] {'ex','feat'}, use_global_device_ids=true, to_apply=%region_14.17 | all-reduce | flops 1 | bytes 8 | tf_op jit(solution)/shard_map/psum | solution.py:74
  348.2 3.2 fusion.42
  353.0 9.5 fusion.8
  362.5 2.9 scatter_custom_fusion.3
  365.4 57.4 %all-reduce.11.cloned.1.call-done = f32[2048,128]{1,0:T(8,128)} async-done(((f32[2048,128]{1,0:T(8,128)}), f32[2048,128]{1,0:T(8,128)}) %all-reduce.11.cloned.1.call-update) | async-done | bytes 1048592 | tf_op jit(solution)/shard_map/psum | solution.py:31
  422.8 2.4 multiply_convert_fusion.1
  425.2 2.3 gather_fusion.4
  427.6 6.4 fusion.6
  434.0 3.3 scatter_custom_fusion.4
  437.4 90.8 %all-reduce.13.cloned.1.call-done = f32[4096,128]{1,0:T(8,128)} async-done(((f32[4096,128]{1,0:T(8,128)}), f32[4096,128]{1,0:T(8,128)}) %all-reduce.13.cloned.1.call-update) | async-done | bytes 2097168 | tf_op jit(solution)/shard_map/psum | solution.py:65
  528.1 3.2 multiply_add_fusion.1
  532.6 1.5 multiply_reduce_fusion.1
  534.1 65.4 %psum.113 = f32[]{:T(128)} all-reduce(f32[]{:T(128)} %multiply_reduce_fusion.1), channel_id=1, replica_groups=mesh['ex'=16,'feat'=8] {'ex','feat'}, use_global_device_ids=true, to_apply=%region_20.23 | all-reduce | flops 1 | bytes 8 | tf_op jit(solution)/shard_map/psum | solution.py:68
  600.8 2.4 multiply_subtract_fusion
  605.2 62.8 %psum.114 = f32[]{:T(128)} all-reduce(f32[]{:T(128)} %multiply_reduce_fusion), channel_id=1, replica_groups=mesh['ex'=16,'feat'=8] {'ex','feat'}, use_global_device_ids=true, to_apply=%region_22.25 | all-reduce | flops 1 | bytes 8 | tf_op jit(solution)/shard_map/psum | solution.py:74
  669.3 4.3 fusion.41
  673.6 2.5 gather_fusion.5
  676.3 9.5 fusion.4
  685.7 2.9 scatter_custom_fusion.5
  688.6 57.5 %all-reduce.15.cloned.1.call-done = f32[2048,128]{1,0:T(8,128)} async-done(((f32[2048,128]{1,0:T(8,128)}), f32[2048,128]{1,0:T(8,128)}) %all-reduce.15.cloned.1.call-update) | async-done | bytes 1048592 | tf_op jit(solution)/shard_map/psum | solution.py:31
  746.2 2.4 multiply_convert_fusion
  748.5 2.3 gather_fusion.6
  750.9 6.4 fusion.2
  757.3 3.3 scatter_custom_fusion.6
  760.6 90.9 %all-reduce.17.cloned.1.call-done = f32[4096,128]{1,0:T(8,128)} async-done(((f32[4096,128]{1,0:T(8,128)}), f32[4096,128]{1,0:T(8,128)}) %all-reduce.17.cloned.1.call-update) | async-done | bytes 2097168 | tf_op jit(solution)/shard_map/psum | solution.py:65
  851.5 1.7 fusion.38
  854.1 65.4 %psum.117 = f32[]{:T(128)} all-reduce(f32[]{:T(128)} %fusion.38), channel_id=1, replica_groups=mesh['ex'=16,'feat'=8] {'ex','feat'}, use_global_device_ids=true, to_apply=%region_28.31 | all-reduce | flops 1 | bytes 8 | tf_op jit(solution)/shard_map/psum | solution.py:68
  920.9 1.7 convert_multiply_fusion
  922.6 1.5 select_reduce_fusion.1
  924.1 12.9 %psum.118 = f32[64]{0:T(128)S(1)} all-reduce(f32[64]{0:T(128)S(1)} %select_reduce_fusion.1), channel_id=1, replica_groups=mesh['ex'=16,'feat'=8] {'feat'}, use_global_device_ids=true, to_apply=%region_30.33 | all-reduce | flops 64 | bytes 512 | tf_op jit(solution)/shard_map/psum | solution.py:98
  937.0 30.6 %psum.119 = f32[64]{0:T(128)S(1)} all-reduce(f32[64]{0:T(128)S(1)} %psum.118), channel_id=1, replica_groups=mesh['ex'=16,'feat'=8] {'ex'}, use_global_device_ids=true, to_apply=%region_31.34 | all-reduce | flops 64 | bytes 512 | tf_op jit(solution)/shard_map/psum | solution.py:98
  (84 shorter events, 36.9 us)
Async XLA Ops:
  7.2 4.1 copy-start.5
  7.2 96.1 %all-reduce.19.cloned.1.call-start = ((), (), s32[]{:S(2)}) async-start(), calls=%async_computation.5 | async-start | bytes 4194304 | tf_op jit(solution)/shard_map/psum | solution.py:31
  8.0 4.7 copy-start.7
  8.0 4.7 copy-start.8
  12.9 10.9 %copy-start = (bf16[1,1,384,128,128]{4,3,2,1,0:T(8,128)(2,1)S(1)}, bf16[1,1,384,128,128]{4,3,2,1,0:T(8,128)(2,1)}, u32[]{:S(2)}) copy-start(bf16[1,1,384,128,128]{4,3,2,1,0:T(8,128)(2,1)} %param.13) | copy-start | bytes 37748740
  36.1 171.3 %all-reduce.9.cloned.1.call-start = ((), (), s32[]{:S(2)}) async-start(), calls=%async_computation | async-start | bytes 4194304 | tf_op jit(solution)/shard_map/psum | solution.py:65
  113.1 3.3 copy-start.6
  116.3 91.1 %copy-start.1 = (f32[4096,128]{1,0:T(8,128)S(1)}, f32[4096,128]{1,0:T(8,128)}, u32[]{:S(2)}) copy-start(f32[4096,128]{1,0:T(8,128)} %param.17) | copy-start | bytes 6291460
  116.3 306.5 %all-reduce.11.cloned.1.call-start = ((), (), s32[]{:S(2)}) async-start(), calls=%async_computation.1 | async-start | bytes 2097152 | tf_op jit(solution)/shard_map/psum | solution.py:31
  362.5 60.4 %copy-start.2 = (f32[2048,128]{1,0:T(8,128)S(1)}, f32[2048,128]{1,0:T(8,128)}, u32[]{:S(2)}) copy-start(f32[2048,128]{1,0:T(8,128)} %get-tuple-element.70) | copy-start | bytes 3145732
  365.4 162.8 %all-reduce.13.cloned.1.call-start = ((), (), s32[]{:S(2)}) async-start(), calls=%async_computation.2 | async-start | bytes 4194304 | tf_op jit(solution)/shard_map/psum | solution.py:65
  437.3 308.8 %all-reduce.15.cloned.1.call-start = ((), (), s32[]{:S(2)}) async-start(), calls=%async_computation.3 | async-start | bytes 2097152 | tf_op jit(solution)/shard_map/psum | solution.py:31
  531.3 1.3 copy-start.4
  603.3 1.3 copy-start.3
  688.6 162.9 %all-reduce.17.cloned.1.call-start = ((), (), s32[]{:S(2)}) async-start(), calls=%async_computation.4 | async-start | bytes 4194304 | tf_op jit(solution)/shard_map/psum | solution.py:65
Sparse Core Ops, SparseCore 0:
  36.2 66.9 all-reduce.18
  116.5 90.8 all-reduce.8
  365.5 57.3 all-reduce.10
  437.4 90.6 all-reduce.12
  688.7 57.3 all-reduce.14
  760.8 90.7 all-reduce.16
